TPU v7x, 256 devices: a whole 4x4x8 slice. The times are simulated.
256 devices in a mesh: layer: 4 (over y), row: 16 (over z, core), col: 4 (over x).
Axes of the slice: x: 4, y: 4, z: 8, core: 2. Of those that a mesh axis runs over, the one named last changes fastest.
Arguments:
- ancestor: float32 [6144, 6144], P('row', 'col'), may hold values from -6 to 6
- leaf_lower: bfloat16 [4, 8, 6144, 512], P('layer', 'col', 'row'), may hold values from -6 to 6
- leaf_upper: bfloat16 [4, 8, 512, 6144], P('layer', None, 'row', 'col'), may hold values from -6 to 6
- leaf_upper_inv: bfloat16 [4, 8, 512, 512], P('layer', 'col'), may hold values from -1 to 1, as said below
- leaf_lower_inv: bfloat16 [4, 8, 512, 512], P('layer'), may hold values from -1 to 2, as said below
- leaf_pivots: int32 [4, 8, 512], P('layer'), may hold values from 0 to 511, each once within a row
- leaf_tiles: int32 [4, 8, 24, 24], P('layer'), may hold values 0 or 1
- anc_upper_inv: bfloat16 [512, 512], replicated, may hold values from -1 to 1, as said below
- anc_lower_inv: bfloat16 [512, 512], replicated, may hold values from -1 to 2, as said below
- anc_pivots: int32 [512], replicated, may hold values from 0 to 511, each once
- anc_tiles: int32 [24, 24], replicated, may hold values 0 or 1
Outputs:
- anc_lower: bfloat16 [6144, 512], P('row')
- anc_upper: bfloat16 [512, 6144], P(None, 'col')
- schur: float32 [6144, 6144], P('row', 'col')
Inputs may be any that keep to these rules, and one draw needn't show every extreme that they name: leaf_upper_inv[l,k] is upper triangular with positive diagonal. leaf_lower_inv[l,k] is lower triangular with positive diagonal. `anc_upper_inv`: upper triangular with positive diagonal. `anc_lower_inv`: lower triangular with positive diagonal.
All inputs are finite; a program needn't handle non-finite values. No bound on the sum of `leaf_tiles` on one device may be relied on, other than what follows from the above.
Results may differ from a plain program's by a relative error of at most 0.0085.
Values may be sent and summed in bfloat16 or wider, within the bound.
A program may use at most 128 MiB of HBM per device.

v0:
```python
import jax
import jax.numpy as jnp
from jax import lax
from jax.sharding import PartitionSpec as P

W = 512
TB = 256
NT = 24


def joined_along(blocks, dim):
    blocks = jnp.moveaxis(blocks, 0, dim)
    lengths = blocks.shape
    return blocks.reshape(*lengths[:dim], lengths[dim] * lengths[dim + 1], *lengths[dim + 2 :])


def sent_to_all(x, axis):
    count = lax.axis_size(axis)
    return lax.all_to_all(jnp.broadcast_to(x[None], (count, *x.shape)), axis, 0, 0, tiled=True)


def gathered_copies(x, axis, dim):
    return joined_along(sent_to_all(x, axis), dim)


def from_root(x, axis, root):
    return lax.dynamic_index_in_dim(lax.all_gather(x, axis), root, 0, keepdims=False)


def onehot_tiles(first, count):
    positions = first + jnp.arange(count, dtype=jnp.int32)
    tile_index = positions // TB
    return (tile_index[:, None] == jnp.arange(NT, dtype=jnp.int32)[None, :]).astype(jnp.float32)


def shards(
    ancestor,
    leaf_lower,
    leaf_upper,
    leaf_upper_inv,
    leaf_lower_inv,
    leaf_pivots,
    leaf_tiles,
    anc_upper_inv,
    anc_lower_inv,
    anc_pivots,
    anc_tiles,
):
    row_count, col_count = ancestor.shape
    panel_rows = leaf_upper.shape[2]
    row_onehot = onehot_tiles(lax.axis_index("row") * row_count, row_count)
    col_onehot = onehot_tiles(lax.axis_index("col") * col_count, col_count)
    upper_local = leaf_upper[0]
    column_share = lax.all_to_all(upper_local, "row", split_axis=2, concat_axis=1, tiled=True)
    permuted = jnp.take_along_axis(column_share, leaf_pivots[0][:, :, None], axis=1)
    finished = jnp.einsum(
        "kij,kjc->kic", leaf_lower_inv[0], permuted, preferred_element_type=jnp.float32
    ).astype(jnp.bfloat16)
    upper_all = lax.all_gather(finished, "row", axis=2, tiled=True)
    own_lower = jnp.einsum(
        "jrw,jwv->jrv", leaf_lower[0], leaf_upper_inv[0], preferred_element_type=jnp.float32
    ).astype(jnp.bfloat16)
    tiles_float = leaf_tiles[0].astype(jnp.float32)
    masks = jnp.einsum("rt,mts,cs->mrc", row_onehot, tiles_float, col_onehot)
    products = jnp.einsum(
        "mrw,mwc->mrc",
        lax.all_gather(own_lower, "col", axis=0, tiled=True),
        upper_all,
        preferred_element_type=jnp.float32,
    )
    contrib = jnp.sum(masks * products, axis=0)
    total = lax.psum(contrib, "layer")
    a_sum = ancestor + total
    local_pivot = a_sum[:panel_rows].astype(jnp.bfloat16)
    gathered = gathered_copies(local_pivot, "row", 0)
    reordered = jnp.take(gathered, anc_pivots, axis=0)
    anc_upper = jnp.dot(anc_lower_inv, reordered, preferred_element_type=jnp.float32).astype(
        jnp.bfloat16
    )
    columns = a_sum[:, :W].astype(jnp.bfloat16)
    panel = jnp.dot(columns, anc_upper_inv, preferred_element_type=jnp.float32).astype(jnp.bfloat16)
    anc_lower = from_root(panel, "col", 0)
    anc_mask = jnp.einsum("rt,ts,cs->rc", row_onehot, anc_tiles.astype(jnp.float32), col_onehot)
    schur = a_sum - anc_mask * jnp.dot(anc_lower, anc_upper, preferred_element_type=jnp.float32)
    return (anc_lower, anc_upper, schur)


def solution(mesh):
    return jax.shard_map(
        shards,
        mesh=mesh,
        in_specs=(
            P("row", "col"),
            P("layer", "col", "row", None),
            P("layer", None, "row", "col"),
            P("layer", "col", None, None),
            P("layer", None, None, None),
            P("layer", None, None),
            P("layer", None, None, None),
            P(),
            P(),
            P(),
            P(),
        ),
        out_specs=(P("row", None), P(None, "col"), P("row", "col")),
        check_vma=False,
    )
```

profile of v0, /device:TPU:1, one launch (start us, length us, event | category | flops | bytes accessed | tf_op | source)
XLA Modules:
  0.0 328.2 jit_solution(1591160123530114196)
XLA Ops:
  8.4 2.6 convolution_convert_fusion.1
  11.0 3.5 %copy.16 = bf16[1,8,32,1536]{2,1,3,0:T(8,128)(2,1)} copy(bf16[1,8,32,1536]{3,2,1,0:T(8,128)(2,1)S(1)} %copy-done.6) | data formatting | bytes 1572864 | tf_op args[2]
  14.5 3.1 bitcast_bitcast_fusion
  17.6 5.7 %reshape.121 = bf16[16,2,12288]{2,1,0:T(2,128)(2,1)} reshape(bf16[1536,8,32]{2,1,0:T(8,128)(2,1)} %bitcast_bitcast_fusion) | data formatting | bytes 1572864
  23.3 10.0 %all-to-all-start = ((bf16[16,2,12288]{2,1,0:T(2,128)(2,1)}), bf16[16,2,12288]{2,1,0:T(2,128)(2,1)S(1)}, u32[]{:S(2)}, u32[]{:S(2)}) async-start(bf16[16,2,12288]{2,1,0:T(2,128)(2,1)} %reshape.121), calls=%async_computation | async-start | bytes 1572864 | tf_op jit(solution)/shard_map/all_to_all | solution.py:54
  33.4 22.6 %all-to-all-done = bf16[16,2,12288]{2,1,0:T(2,128)(2,1)S(1)} async-done(((bf16[16,2,12288]{2,1,0:T(2,128)(2,1)}), bf16[16,2,12288]{2,1,0:T(2,128)(2,1)S(1)}, u32[]{:S(2)}, u32[]{:S(2)}) %all-to-all-start) | async-done | bytes 786464 | tf_op jit(solution)/shard_map/all_to_all | solution.py:54
  56.0 2.7 reshape.122
  58.7 3.9 %copy.17 = bf16[8,32,16,96]{3,1,2,0:T(8,128)(2,1)S(1)} copy(bf16[8,32,16,96]{1,0,3,2:T(8,128)(2,1)} %bitcast.62) | data formatting | bytes 1572864 | tf_op jit(solution)/shard_map/all_to_all | solution.py:54
  62.6 21.7 %gather_fusion.1 = bf16[4096,96]{1,0:T(8,128)(2,1)S(1)} fusion(bf16[8,512,96]{2,1,0:T(8,128)(2,1)S(1)} %bitcast.61, s32[4096]{0:T(1024)S(1)} %bitcast.59), kind=kCustom, calls=%fused_computation.1 | custom fusion | bytes 1605632 | tf_op jit(solution)/shard_map/jit(take_along_axis)/gather | solution.py:55
  84.3 4.5 %fusion.8 = bf16[8,512,96]{1,2,0:T(8,128)(2,1)} fusion(bf16[1,8,512,512]{3,2,1,0:T(8,128)(2,1)} %param.15, bf16[8,512,96]{2,1,0:T(8,128)(2,1)S(1)} %bitcast.64, pred[8,512]{1,0:T(8,128)(4,1)S(1)} %compare_and_fusion), kind=kOutput, calls=%fused_computation.12 | convolution fusion | flops 403439616 | bytes 5771264 | tf_op jit(solution)/shard_map/kij,kjc->kic/dot_general | solution.py:56
  88.9 72.9 %all-gather.7.cloned.1.call-done = bf16[8,512,1536]{1,2,0:T(8,128)(2,1)} async-done(((bf16[8,512,96]{1,2,0:T(8,128)(2,1)}), bf16[8,512,1536]{1,2,0:T(8,128)(2,1)}) %all-gather.7.cloned.1.call-update) | async-done | bytes 12582928 | tf_op jit(solution)/shard_map/all_gather | solution.py:59
  161.8 17.2 %fusion.50 = f32[8,384,1536]{2,1,0:T(8,128)} fusion(bf16[8,384,512]{2,1,0:T(8,128)(2,1)} %all-gather.5.cloned.1.call-done, bf16[8,512,1536]{1,2,0:T(8,128)(2,1)} %all-gather.7.cloned.1.call-done), kind=kOutput, calls=%fused_computation.66 | convolution fusion | flops 4831838208 | bytes 34603008 | tf_op jit(solution)/shard_map/mrw,mwc->mrc/dot_general | solution.py:65
  179.1 9.6 %multiply_reduce_fusion = f32[384,1536]{1,0:T(8,128)} fusion(f32[8,384,1536]{2,1,0:T(8,128)} %fusion.50, s32[1,8,24,24]{3,2,1,0:T(8,128)S(1)} %copy-done.7, s32[384]{0:T(512)S(1)} %add_select_fusion.1, s32[1536]{0:T(1024)S(1)} %add_select_fusion), kind=kOutput, calls=%fused_computation.2 | convolution fusion | flops 238929408 | bytes 21259776 | tf_op jit(solution)/shard_map/rt,mts,cs->mrc/dot_general | solution.py:64
  188.7 66.2 %all-reduce.2.cloned.1.call-done = f32[384,1536]{1,0:T(8,128)} async-done(((f32[384,1536]{1,0:T(8,128)}), f32[384,1536]{1,0:T(8,128)}) %all-reduce.2.cloned.1.call-update) | async-done | bytes 2359312 | tf_op jit(solution)/shard_map/psum | solution.py:72
  254.9 3.6 %fusion.49 = (bf16[384,1536]{1,0:T(8,128)(2,1)S(1)}, f32[384,1536]{1,0:T(8,128)}) fusion(f32[384,1536]{1,0:T(8,128)S(1)} %copy-done.3, f32[384,1536]{1,0:T(8,128)} %all-reduce.2.cloned.1.call-done), kind=kLoop, calls=%fused_computation.64 | loop fusion | flops 1179648 | bytes 8257536 | tf_op jit(solution)/shard_map/convert.1
  260.8 8.0 %all-to-all-start.1 = ((bf16[16,32,1536]{2,1,0:T(8,128)(2,1)}), bf16[16,32,1536]{2,1,0:T(8,128)(2,1)S(1)}, u32[]{:S(2)}, u32[]{:S(2)}) async-start(bf16[16,32,1536]{2,1,0:T(8,128)(2,1)} %broadcast_in_dim.33), calls=%async_computation.1 | async-start | bytes 3145728 | tf_op jit(solution)/shard_map/all_to_all | solution.py:19
  269.0 2.1 convolution_convert_fusion.2
  271.2 28.6 %all-gather.9.cloned.1.call-done = bf16[1536,512]{1,0:T(8,128)(2,1)} async-done(((bf16[384,512]{1,0:T(8,128)(2,1)}), bf16[1536,512]{1,0:T(8,128)(2,1)}) %all-gather.9.cloned.1.call-update) | async-done | bytes 1572880 | tf_op jit(solution)/shard_map/all_gather | solution.py:27
  300.9 6.4 %all-to-all-done.1 = bf16[16,32,1536]{2,1,0:T(8,128)(2,1)S(1)} async-done(((bf16[16,32,1536]{2,1,0:T(8,128)(2,1)}), bf16[16,32,1536]{2,1,0:T(8,128)(2,1)S(1)}, u32[]{:S(2)}, u32[]{:S(2)}) %all-to-all-start.1) | async-done | bytes 1572896 | tf_op jit(solution)/shard_map/all_to_all | solution.py:19
  307.3 2.9 gather_fusion
  310.2 2.6 convolution_convert_fusion
  314.0 1.6 copy.18
  315.6 2.2 fusion.51
  317.8 3.8 %fusion.2 = f32[384,1536]{1,0:T(8,128)} fusion(f32[384,1536]{1,0:T(8,128)} %get-tuple-element.10, f32[384,1536]{1,0:T(8,128)S(1)} %fusion.51, s32[384]{0:T(512)S(1)} %add_select_fusion.1, s32[1536]{0:T(1024)S(1)} %add_select_fusion, s32[24,24]{1,0:T(8,128)S(1)} %copy-done.9), kind=kOutput, calls=%fused_computation.6 | convolution fusion | flops 29980224 | bytes 7087872 | tf_op jit(solution)/shard_map/rt,ts,cs->rc/dot_general | solution.py:83
  (46 shorter events, 6.2 us)
Async XLA Ops:
  7.2 1.2 copy-start
  7.2 3.8 %copy-start.6 = (bf16[1,8,32,1536]{3,2,1,0:T(8,128)(2,1)S(1)}, bf16[1,8,32,1536]{3,2,1,0:T(8,128)(2,1)}, u32[]{:S(2)}) copy-start(bf16[1,8,32,1536]{3,2,1,0:T(8,128)(2,1)} %param.13) | copy-start | bytes 2359300
  7.2 81.7 %all-gather.5.cloned.1.call-start = ((), (), s32[]{:S(2)}) async-start(), calls=%async_computation.2 | async-start | bytes 3932160 | tf_op jit(solution)/shard_map/all_gather | solution.py:67
  17.6 15.7 %copy-start.8 = (s32[1,8,512]{2,1,0:T(8,128)S(1)}, s32[1,8,512]{2,1,0:T(8,128)}, u32[]{:S(2)}) copy-start(s32[1,8,512]{2,1,0:T(8,128)} %param.16) | copy-start | bytes 49156
  23.3 32.7 %all-to-all-start = ((bf16[16,2,12288]{2,1,0:T(2,128)(2,1)}), bf16[16,2,12288]{2,1,0:T(2,128)(2,1)S(1)}, u32[]{:S(2)}, u32[]{:S(2)}) async-start(bf16[16,2,12288]{2,1,0:T(2,128)(2,1)} %reshape.121), calls=%async_computation | async-start | bytes 1572864 | tf_op jit(solution)/shard_map/all_to_all | solution.py:54
  33.3 128.5 %all-gather.7.cloned.1.call-start = ((), (), s32[]{:S(2)}) async-start(), calls=%async_computation.3 | async-start | bytes 13369344 | tf_op jit(solution)/shard_map/all_gather | solution.py:59
  88.8 166.1 %all-reduce.2.cloned.1.call-start = ((), (), s32[]{:S(2)}) async-start(), calls=%async_computation.4 | async-start | bytes 4718592 | tf_op jit(solution)/shard_map/psum | solution.py:72
  88.9 90.2 %copy-start.7 = (s32[1,8,24,24]{3,2,1,0:T(8,128)S(1)}, s32[1,8,24,24]{3,2,1,0:T(8,128)}, u32[]{:S(2)}) copy-start(s32[1,8,24,24]{3,2,1,0:T(8,128)} %param.17) | copy-start | bytes 55300
  188.7 66.2 %copy-start.3 = (f32[384,1536]{1,0:T(8,128)S(1)}, f32[384,1536]{1,0:T(8,128)}, u32[]{:S(2)}) copy-start(f32[384,1536]{1,0:T(8,128)} %param.11) | copy-start | bytes 7077892
  258.4 1.0 copy-start.5
  259.5 9.5 %copy-start.11 = (bf16[512,512]{1,0:T(8,128)(2,1)S(1)}, bf16[512,512]{1,0:T(8,128)(2,1)}, u32[]{:S(2)}) copy-start(bf16[512,512]{1,0:T(8,128)(2,1)} %param.18) | copy-start | bytes 1572868
  260.8 10.4 %copy-start.10 = (s32[512]{0:T(512)S(1)}, s32[512]{0:T(512)}, u32[]{:S(2)}) copy-start(s32[512]{0:T(512)} %param.20) | copy-start | bytes 6148
  260.8 46.5 %all-to-all-start.1 = ((bf16[16,32,1536]{2,1,0:T(8,128)(2,1)}), bf16[16,32,1536]{2,1,0:T(8,128)(2,1)S(1)}, u32[]{:S(2)}, u32[]{:S(2)}) async-start(bf16[16,32,1536]{2,1,0:T(8,128)(2,1)} %broadcast_in_dim.33), calls=%async_computation.1 | async-start | bytes 3145728 | tf_op jit(solution)/shard_map/all_to_all | solution.py:19
  268.8 31.1 %all-gather.9.cloned.1.call-start = ((), (), s32[]{:S(2)}) async-start(), calls=%async_computation.5 | async-start | bytes 1966080 | tf_op jit(solution)/shard_map/all_gather | solution.py:27
  300.9 14.7 %copy-start.4 = (bf16[384,512]{1,0:T(8,128)(2,1)}, bf16[384,512]{1,0:T(8,128)(2,1)S(1)}, u32[]{:S(2)}) copy-start(bf16[384,512]{1,0:T(8,128)(2,1)S(1)} %slice.17) | copy-start | bytes 1179652
  307.3 2.9 copy-start.12
  312.9 1.2 copy-start.2
  315.6 2.2 copy-start.9
  317.8 3.8 %copy-start.1 = (bf16[1,2,512,512]{3,2,1,0:T(8,128)(2,1)S(1)}, bf16[1,2,512,512]{3,2,1,0:T(8,128)(2,1)}, u32[]{:S(2)}) copy-start(bf16[1,2,512,512]{3,2,1,0:T(8,128)(2,1)} %param.14) | copy-start | bytes 3145732
Sparse Core Ops, SparseCore 0:
  11.1 45.6 all-gather.4
  88.9 72.8 all-gather.6
  188.8 66.0 all-reduce.1
  271.7 28.1 all-gather.8
where the time goes:
time: 329 us; the launch traced here: 328 us
  waiting for transfers between devices  197 us (60%)
  local copies, waits for them, and re-layouts  50.8 us (15%)
  matrix products  44.6 us (14%)
  starting transfers between devices  18.3 us (6%)
  between operations  14 us (4%)
  other arithmetic  3.63 us (1%)
    all_gather x1, waiting for transfers between devices, shards(): upper_all = lax.all_gather(finished, 'row', axis=2, tiled=True)  72.9 us
    psum x1, waiting for transfers between devices, shards(): total = lax.psum(contrib, 'layer')  66.2 us
    all_gather x1, waiting for transfers between devices, from_root(): lax.all_gather(x, axis)  28.6 us
    all_to_all x1, waiting for transfers between devices, shards(): lax.all_to_all(upper_local, 'row', split_axis=2, concat_axis=1, tiled=True)  22.6 us
    gather x1, local copies, waits for them, and re-layouts, shards(): jnp.take_along_axis(column_share, leaf_pivots[0][:, :, None], axis=1)  21.7 us
    unnamed x32, local copies, waits for them, and re-layouts  19.9 us
    dot_general x1, matrix products, shards(): jnp.einsum('mrw,mwc->mrc', lax.all_gather(own_lower, 'col', axis=0, tiled...  17.2 us
    all_to_all x1, starting transfers between devices, shards(): lax.all_to_all(upper_local, 'row', split_axis=2, concat_axis=1, tiled=True)  9.97 us
  transfers between devices with their start and end apart: 6, of which 5 were waited for; matrix products, arithmetic and copies ran while one was open for 15% of the time, Pallas kernels for 0%

commit v1 on v0

--- a/solution.py
+++ b/solution.py
@@ -69,7 +69,9 @@
         preferred_element_type=jnp.float32,
     )
     contrib = jnp.sum(masks * products, axis=0)
-    total = lax.psum(contrib, "layer")
+    total = contrib
+    for hop in (1, 2):
+        total = total + lax.ppermute(total, "layer", [(dev, dev ^ hop) for dev in range(4)])
     a_sum = ancestor + total
     local_pivot = a_sum[:panel_rows].astype(jnp.bfloat16)
     gathered = gathered_copies(local_pivot, "row", 0)

time: 329 us -> 367 us (1.12)
  waiting for transfers between devices: 197 us -> 233 us
    ppermute x0 -> x2, waiting for transfers between devices: none -> 102 us  [shards(): lax.ppermute(total, 'layer', [(dev, dev ^ hop) for dev in range(4)])]
    psum x1 -> x0, waiting for transfers between devices: 66.2 us -> none  [shards(): total = lax.psum(contrib, 'layer')]
    ppermute x0 -> x2, starting transfers between devices: none -> 4.29 us  [shards(): lax.ppermute(total, 'layer', [(dev, dev ^ hop) for dev in range(4)])]
    unnamed x32 -> x38, local copies, waits for them, and re-layouts: 19.9 us -> 20.6 us
  transfers between devices with their start and end apart: 6 -> 7, of which waited for: 5 -> 6; matrix products, arithmetic and copies ran while one was open for 15% -> 13% of each run, Pallas kernels for 0% -> 0%
where the time goes in v1:
time: 367 us; the launch traced here: 366 us
  waiting for transfers between devices  233 us (63%)
  local copies, waits for them, and re-layouts  51.4 us (14%)
  matrix products  46.3 us (13%)
  starting transfers between devices  20.7 us (6%)
  between operations  14 us (4%)
    ppermute x2, waiting for transfers between devices, shards(): lax.ppermute(total, 'layer', [(dev, dev ^ hop) for dev in range(4)])  102 us
    all_gather x1, waiting for transfers between devices, shards(): upper_all = lax.all_gather(finished, 'row', axis=2, tiled=True)  73 us
    all_gather x1, waiting for transfers between devices, from_root(): lax.all_gather(x, axis)  30.6 us
    all_to_all x1, waiting for transfers between devices, shards(): lax.all_to_all(upper_local, 'row', split_axis=2, concat_axis=1, tiled=True)  22.6 us
    gather x1, local copies, waits for them, and re-layouts, shards(): jnp.take_along_axis(column_share, leaf_pivots[0][:, :, None], axis=1)  21.7 us
    unnamed x38, local copies, waits for them, and re-layouts  20.6 us
    dot_general x1, matrix products, shards(): jnp.einsum('mrw,mwc->mrc', lax.all_gather(own_lower, 'col', axis=0, tiled...  17.2 us
    all_to_all x1, starting transfers between devices, shards(): lax.all_to_all(upper_local, 'row', split_axis=2, concat_axis=1, tiled=True)  9.97 us
  transfers between devices with their start and end apart: 7, of which 6 were waited for; matrix products, arithmetic and copies ran while one was open for 13% of the time, Pallas kernels for 0%

profile of v1, /device:TPU:1, one launch (start us, length us, event | category | flops | bytes accessed | tf_op | source)
XLA Modules:
  0.0 366.4 jit_solution(3402713762394614920)
XLA Ops:
  8.4 2.6 convolution_convert_fusion.1
  11.0 3.5 copy.16
  14.5 3.1 bitcast_bitcast_fusion
  17.6 5.7 %reshape.121 = bf16[16,2,12288]{2,1,0:T(2,128)(2,1)} reshape(bf16[1536,8,32]{2,1,0:T(8,128)(2,1)} %bitcast_bitcast_fusion) | data formatting | bytes 1572864
  23.4 10.0 %all-to-all-start = ((bf16[16,2,12288]{2,1,0:T(2,128)(2,1)}), bf16[16,2,12288]{2,1,0:T(2,128)(2,1)S(1)}, u32[]{:S(2)}, u32[]{:S(2)}) async-start(bf16[16,2,12288]{2,1,0:T(2,128)(2,1)} %reshape.121), calls=%async_computation | async-start | bytes 1572864 | tf_op jit(solution)/shard_map/all_to_all | solution.py:54
  33.4 22.6 %all-to-all-done = bf16[16,2,12288]{2,1,0:T(2,128)(2,1)S(1)} async-done(((bf16[16,2,12288]{2,1,0:T(2,128)(2,1)}), bf16[16,2,12288]{2,1,0:T(2,128)(2,1)S(1)}, u32[]{:S(2)}, u32[]{:S(2)}) %all-to-all-start) | async-done | bytes 786464 | tf_op jit(solution)/shard_map/all_to_all | solution.py:54
  56.0 2.7 reshape.122
  58.7 3.9 %copy.17 = bf16[8,32,16,96]{3,1,2,0:T(8,128)(2,1)S(1)} copy(bf16[8,32,16,96]{1,0,3,2:T(8,128)(2,1)} %bitcast.62) | data formatting | bytes 1572864 | tf_op jit(solution)/shard_map/all_to_all | solution.py:54
  62.6 21.7 %gather_fusion.1 = bf16[4096,96]{1,0:T(8,128)(2,1)S(1)} fusion(bf16[8,512,96]{2,1,0:T(8,128)(2,1)S(1)} %bitcast.61, s32[4096]{0:T(1024)S(1)} %bitcast.59), kind=kCustom, calls=%fused_computation.1 | custom fusion | bytes 1605632 | tf_op jit(solution)/shard_map/jit(take_along_axis)/gather | solution.py:55
  84.3 4.5 %fusion.8 = bf16[8,512,96]{1,2,0:T(8,128)(2,1)} fusion(bf16[1,8,512,512]{3,2,1,0:T(8,128)(2,1)} %param.15, bf16[8,512,96]{2,1,0:T(8,128)(2,1)S(1)} %bitcast.64, pred[8,512]{1,0:T(8,128)(4,1)S(1)} %compare_and_fusion), kind=kOutput, calls=%fused_computation.13 | convolution fusion | flops 403439616 | bytes 5771264 | tf_op jit(solution)/shard_map/kij,kjc->kic/dot_general | solution.py:56
  88.9 73.0 %all-gather.7.cloned.1.call-done = bf16[8,512,1536]{1,2,0:T(8,128)(2,1)} async-done(((bf16[8,512,96]{1,2,0:T(8,128)(2,1)}), bf16[8,512,1536]{1,2,0:T(8,128)(2,1)}) %all-gather.7.cloned.1.call-update) | async-done | bytes 12582928 | tf_op jit(solution)/shard_map/all_gather | solution.py:59
  161.9 17.2 %fusion.50 = f32[8,384,1536]{2,1,0:T(8,128)} fusion(bf16[8,384,512]{2,1,0:T(8,128)(2,1)} %all-gather.5.cloned.1.call-done, bf16[8,512,1536]{1,2,0:T(8,128)(2,1)} %all-gather.7.cloned.1.call-done), kind=kOutput, calls=%fused_computation.67 | convolution fusion | flops 4831838208 | bytes 34603008 | tf_op jit(solution)/shard_map/mrw,mwc->mrc/dot_general | solution.py:65
  179.1 8.2 %multiply_reduce_fusion = f32[384,1536]{1,0:T(8,128)S(1)} fusion(f32[8,384,1536]{2,1,0:T(8,128)} %fusion.50, s32[1,8,24,24]{3,2,1,0:T(8,128)S(1)} %copy-done.10, s32[384]{0:T(512)S(1)} %add_select_fusion.1, s32[1536]{0:T(1024)S(1)} %add_select_fusion), kind=kOutput, calls=%fused_computation.2 | convolution fusion | flops 238929408 | bytes 21259776 | tf_op jit(solution)/shard_map/rt,mts,cs->mrc/dot_general | solution.py:64
  188.6 51.3 %collective-permute-done = f32[384,1536]{1,0:T(8,128)S(1)} collective-permute-done((f32[384,1536]{1,0:T(8,128)S(1)}, f32[384,1536]{1,0:T(8,128)S(1)}, u32[]{:S(2)}, u32[]{:S(2)}) %collective-permute-start) | collective-permute-done | bytes 2359328 | tf_op jit(solution)/shard_map/ppermute | solution.py:74
  240.3 3.0 collective-permute-start.1
  243.3 50.5 %collective-permute-done.1 = f32[384,1536]{1,0:T(8,128)S(1)} collective-permute-done((f32[384,1536]{1,0:T(8,128)S(1)}, f32[384,1536]{1,0:T(8,128)S(1)}, u32[]{:S(2)}, u32[]{:S(2)}) %collective-permute-start.1) | collective-permute-done | bytes 2359328 | tf_op jit(solution)/shard_map/ppermute | solution.py:74
  297.5 6.4 %all-to-all-start.1 = ((bf16[16,32,1536]{2,1,0:T(8,128)(2,1)}), bf16[16,32,1536]{2,1,0:T(8,128)(2,1)S(1)}, u32[]{:S(2)}, u32[]{:S(2)}) async-start(bf16[16,32,1536]{2,1,0:T(8,128)(2,1)} %broadcast_in_dim.33), calls=%async_computation.1 | async-start | bytes 3145728 | tf_op jit(solution)/shard_map/all_to_all | solution.py:19
  304.0 2.1 convolution_convert_fusion.2
  306.1 30.6 %all-gather.9.cloned.1.call-done = bf16[1536,512]{1,0:T(8,128)(2,1)} async-done(((bf16[384,512]{1,0:T(8,128)(2,1)}), bf16[1536,512]{1,0:T(8,128)(2,1)}) %all-gather.9.cloned.1.call-update) | async-done | bytes 1572880 | tf_op jit(solution)/shard_map/all_gather | solution.py:27
  337.8 4.6 %all-to-all-done.1 = bf16[16,32,1536]{2,1,0:T(8,128)(2,1)S(1)} async-done(((bf16[16,32,1536]{2,1,0:T(8,128)(2,1)}), bf16[16,32,1536]{2,1,0:T(8,128)(2,1)S(1)}, u32[]{:S(2)}, u32[]{:S(2)}) %all-to-all-start.1) | async-done | bytes 1572896 | tf_op jit(solution)/shard_map/all_to_all | solution.py:19
  342.4 2.9 gather_fusion
  345.4 2.6 convolution_convert_fusion
  350.8 3.8 %fusion.51 = f32[384,1536]{1,0:T(8,128)} fusion(bf16[384,512]{1,0:T(8,128)(2,1)S(1)} %slice.17, bf16[1536,512]{1,0:T(8,128)(2,1)} %copy-done.6), kind=kOutput, calls=%fused_computation.68 | convolution fusion | flops 603979776 | bytes 4325376 | tf_op jit(solution)/shard_map/dot_general | solution.py:86
  354.5 5.3 %fusion.2 = f32[384,1536]{1,0:T(8,128)} fusion(f32[384,1536]{1,0:T(8,128)} %fusion.51, s32[384]{0:T(512)S(1)} %add_select_fusion.1, s32[1536]{0:T(1024)S(1)} %add_select_fusion, s32[24,24]{1,0:T(8,128)S(1)} %copy-done.12, f32[384,1536]{1,0:T(8,128)} %param.11, f32[384,1536]{1,0:T(8,128)S(1)} %copy-done.3, f32[384,1536]{1,0:T(8,128)} %copy-done.5), kind=kOutput, calls=%fused_computation.6 | convolution fusion | flops 31159872 | bytes 11806464 | tf_op jit(solution)/shard_map/rt,ts,cs->rc/dot_general | solution.py:85
  (54 shorter events, 10.7 us)
Async XLA Ops:
  7.2 1.2 copy-start
  7.2 3.8 %copy-start.9 = (bf16[1,8,32,1536]{3,2,1,0:T(8,128)(2,1)S(1)}, bf16[1,8,32,1536]{3,2,1,0:T(8,128)(2,1)}, u32[]{:S(2)}) copy-start(bf16[1,8,32,1536]{3,2,1,0:T(8,128)(2,1)} %param.13) | copy-start | bytes 2359300
  7.2 81.7 %all-gather.5.cloned.1.call-start = ((), (), s32[]{:S(2)}) async-start(), calls=%async_computation.2 | async-start | bytes 3932160 | tf_op jit(solution)/shard_map/all_gather | solution.py:67
  17.6 15.7 %copy-start.11 = (s32[1,8,512]{2,1,0:T(8,128)S(1)}, s32[1,8,512]{2,1,0:T(8,128)}, u32[]{:S(2)}) copy-start(s32[1,8,512]{2,1,0:T(8,128)} %param.16) | copy-start | bytes 49156
  23.4 32.7 %all-to-all-start = ((bf16[16,2,12288]{2,1,0:T(2,128)(2,1)}), bf16[16,2,12288]{2,1,0:T(2,128)(2,1)S(1)}, u32[]{:S(2)}, u32[]{:S(2)}) async-start(bf16[16,2,12288]{2,1,0:T(2,128)(2,1)} %reshape.121), calls=%async_computation | async-start | bytes 1572864 | tf_op jit(solution)/shard_map/all_to_all | solution.py:54
  33.3 128.5 %all-gather.7.cloned.1.call-start = ((), (), s32[]{:S(2)}) async-start(), calls=%async_computation.3 | async-start | bytes 13369344 | tf_op jit(solution)/shard_map/all_gather | solution.py:59
  88.8 90.2 %copy-start.10 = (s32[1,8,24,24]{3,2,1,0:T(8,128)S(1)}, s32[1,8,24,24]{3,2,1,0:T(8,128)}, u32[]{:S(2)}) copy-start(s32[1,8,24,24]{3,2,1,0:T(8,128)} %param.17) | copy-start | bytes 55300
  187.3 106.5 %copy-start.4 = (f32[384,1536]{1,0:T(8,128)S(1)}, f32[384,1536]{1,0:T(8,128)}, u32[]{:S(2)}) copy-start(f32[384,1536]{1,0:T(8,128)} %param.11) | copy-start | bytes 7077892
  187.3 52.6 %collective-permute-start = (f32[384,1536]{1,0:T(8,128)S(1)}, f32[384,1536]{1,0:T(8,128)S(1)}, u32[]{:S(2)}, u32[]{:S(2)}) collective-permute-start(f32[384,1536]{1,0:T(8,128)S(1)} %multiply_reduce_fusion), channel_id=1, source_target_pairs={{0,64},{64,0},{128,192},{192,128},{1,65},{65,1},{129,193},{193,129... | collective-permute-start | bytes 7077896 | tf_op jit(solution)/shard_map/ppermute | solution.py:74
  240.3 54.3 %copy-start.2 = (f32[384,1536]{1,0:T(8,128)}, f32[384,1536]{1,0:T(8,128)S(1)}, u32[]{:S(2)}) copy-start(f32[384,1536]{1,0:T(8,128)S(1)} %add.79) | copy-start | bytes 7077892
  240.3 53.5 %collective-permute-start.1 = (f32[384,1536]{1,0:T(8,128)S(1)}, f32[384,1536]{1,0:T(8,128)S(1)}, u32[]{:S(2)}, u32[]{:S(2)}) collective-permute-start(f32[384,1536]{1,0:T(8,128)S(1)} %add.79), channel_id=1, source_target_pairs={{0,128},{64,192},{128,0},{192,64},{1,129},{65,193},{129,1},{193,65... | collective-permute-start | bytes 7077896 | tf_op jit(solution)/shard_map/ppermute | solution.py:74
  293.8 1.4 copy-start.5
  295.2 1.0 copy-start.8
  296.2 7.7 %copy-start.14 = (bf16[512,512]{1,0:T(8,128)(2,1)S(1)}, bf16[512,512]{1,0:T(8,128)(2,1)}, u32[]{:S(2)}) copy-start(bf16[512,512]{1,0:T(8,128)(2,1)} %param.18) | copy-start | bytes 1572868
  297.5 8.6 %copy-start.13 = (s32[512]{0:T(512)S(1)}, s32[512]{0:T(512)}, u32[]{:S(2)}) copy-start(s32[512]{0:T(512)} %param.20) | copy-start | bytes 6148
  297.5 44.9 %all-to-all-start.1 = ((bf16[16,32,1536]{2,1,0:T(8,128)(2,1)}), bf16[16,32,1536]{2,1,0:T(8,128)(2,1)S(1)}, u32[]{:S(2)}, u32[]{:S(2)}) async-start(bf16[16,32,1536]{2,1,0:T(8,128)(2,1)} %broadcast_in_dim.33), calls=%async_computation.1 | async-start | bytes 3145728 | tf_op jit(solution)/shard_map/all_to_all | solution.py:19
  303.9 32.9 %all-gather.9.cloned.1.call-start = ((), (), s32[]{:S(2)}) async-start(), calls=%async_computation.4 | async-start | bytes 1966080 | tf_op jit(solution)/shard_map/all_gather | solution.py:27
  337.8 13.0 %copy-start.7 = (bf16[384,512]{1,0:T(8,128)(2,1)}, bf16[384,512]{1,0:T(8,128)(2,1)S(1)}, u32[]{:S(2)}) copy-start(bf16[384,512]{1,0:T(8,128)(2,1)S(1)} %slice.17) | copy-start | bytes 1179652
  342.4 2.9 copy-start.15
  348.0 1.2 copy-start.6
  350.8 3.8 %copy-start.3 = (f32[384,1536]{1,0:T(8,128)S(1)}, f32[384,1536]{1,0:T(8,128)}, u32[]{:S(2)}) copy-start(f32[384,1536]{1,0:T(8,128)} %copy-done.2) | copy-start | bytes 7077892
  350.8 3.8 %copy-start.12 = (s32[24,24]{1,0:T(8,128)S(1)}, s32[24,24]{1,0:T(8,128)}, u32[]{:S(2)}) copy-start(s32[24,24]{1,0:T(8,128)} %param.21) | copy-start | bytes 6916
  354.5 5.3 %copy-start.1 = (bf16[1,2,512,512]{3,2,1,0:T(8,128)(2,1)S(1)}, bf16[1,2,512,512]{3,2,1,0:T(8,128)(2,1)}, u32[]{:S(2)}) copy-start(bf16[1,2,512,512]{3,2,1,0:T(8,128)(2,1)} %param.14) | copy-start | bytes 3145732
Sparse Core Ops, SparseCore 0:
  11.1 45.6 all-gather.4
  88.9 72.8 all-gather.6
  307.1 29.6 all-gather.8
